TPU v7x, 32 devices: a whole 2x2x4 slice. The times are simulated.
32 devices in a mesh: seq: 8 (over z, y), wsh: 4 (over x, core).
Axes of the slice: x: 2, y: 2, z: 4, core: 2. Of those that a mesh axis runs over, the one named last changes fastest.
Arguments:
- layer_input: bfloat16 [4096, 1152], P(('seq', 'wsh')), may hold values from -6 to 6
- w_qkv: bfloat16 [1152, 1536], P('wsh'), may hold values from -0.1875 to 0.1875
- w_out: bfloat16 [1152, 1024], P('wsh'), may hold values from -0.1875 to 0.1875
- w_gate_up: bfloat16 [1152, 6912], P('wsh'), may hold values from -0.1875 to 0.1875
- w_down: bfloat16 [1152, 3456], P('wsh'), may hold values from -0.109375 to 0.109375
- norm_gain: bfloat16 [4, 1152], P(None, 'wsh'), may hold values from 0.099609375 to 1.8984375
- qk_gain: bfloat16 [512], P('wsh'), may hold values from 0.099609375 to 1.8984375
- cotangent: bfloat16 [4096, 1152], P(('seq', 'wsh')), may hold values from -6 to 6
Outputs:
- output: bfloat16 [4096, 1152], P(('seq', 'wsh'))
- grad_input: float32 [4096, 1152], P(('seq', 'wsh'))
- grad_w_qkv: float32 [1152, 1536], P('wsh')
- grad_w_out: float32 [1152, 1024], P('wsh')
- grad_w_gate_up: float32 [1152, 6912], P('wsh')
- grad_w_down: float32 [1152, 3456], P('wsh')
- grad_norm_gain: float32 [4, 1152], P(None, 'wsh')
- grad_qk_gain: float32 [512], P('wsh')
All inputs are finite; a program needn't handle non-finite values.
Results may differ from a plain program's by a relative error of at most 0.024.
Values may be sent and summed in bfloat16 or wider, within the bound.
No kernel may reach another device: no remote copies, remote signals or barrier semaphores. Data moves between devices by JAX's collectives and lax.ppermute only.
A program may use at most 192 MiB of HBM per device.

v0:
```python
import jax
import jax.numpy as jnp
from jax import lax
from jax.sharding import PartitionSpec as P

WIN = 512
EPSILON = 1e-06
GELU_COEF = 0.7978845608028654


def from_behind(value, axis, by):
    peers = lax.axis_size(axis)
    pairs = [(i, i + by) for i in range(peers) if 0 <= i + by < peers]
    return lax.ppermute(value, axis, pairs)


def gelu_tanh(values):
    return (
        0.5 * values * (1.0 + jnp.tanh(GELU_COEF * (values + 0.044715 * values * values * values)))
    )


def gelu_slope(values):
    bend = jnp.tanh(GELU_COEF * (values + 0.044715 * values * values * values))
    return 0.5 * (1.0 + bend) + 0.5 * values * (1.0 - bend * bend) * GELU_COEF * (
        1.0 + 3.0 * 0.044715 * values * values
    )


def inv_rms(values):
    return lax.rsqrt(jnp.mean(values * values, -1, keepdims=True) + EPSILON)


def norm_back(grad_out, values, scale, gain):
    normed = values * scale
    scaled = grad_out * gain
    grad_in = scale * (scaled - normed * jnp.mean(scaled * normed, -1, keepdims=True))
    return (grad_in, grad_out * normed)


def rope_tables(positions, head_dim):
    half = head_dim // 2
    freqs = 10000.0 ** (-(jnp.arange(half, dtype=jnp.float32) * 2.0 / head_dim))
    angles = positions.astype(jnp.float32)[:, None] * freqs[None, :]
    cosine = jnp.cos(angles)
    sine = jnp.sin(angles)
    return (jnp.concatenate([cosine, cosine], -1), jnp.concatenate([sine, sine], -1))


def rotate(values, cosine, sine):
    half = values.shape[-1] // 2
    turned = jnp.concatenate([-values[..., half:], values[..., :half]], -1)
    return values * cosine + turned * sine


def unrotate(grads, cosine, sine):
    half = grads.shape[-1] // 2
    scaled = grads * sine
    turned = jnp.concatenate([scaled[..., half:], -scaled[..., :half]], -1)
    return grads * cosine + turned


def block_mask(query_pos, key_pos):
    gap = query_pos[:, None] - key_pos[None, :]
    return (gap >= 0) & (gap < WIN) & (key_pos[None, :] >= 0)


def outer_sum(left, right):
    return lax.dot_general(
        left, right, (((0,), (0,)), ((), ())), preferred_element_type=jnp.float32
    )


def attend(query_s, keys, mask):
    head_dim = query_s.shape[-1]
    scores = jnp.einsum(
        "qhd,kd->hqk", query_s, keys[:, :head_dim], preferred_element_type=jnp.float32
    )
    exps = jnp.where(mask[None], jnp.exp(scores), 0.0)
    total = jnp.sum(exps, -1, keepdims=True)
    weights = (exps / total).astype(jnp.bfloat16)
    out = jnp.einsum("hqk,kd->qhd", weights, keys[:, head_dim:], preferred_element_type=jnp.float32)
    return (out, jnp.log(total))


def attend_back(query_s, keys, mask, out, log_total, grad_out):
    head_dim = query_s.shape[-1]
    scores = jnp.einsum(
        "qhd,kd->hqk", query_s, keys[:, :head_dim], preferred_element_type=jnp.float32
    )
    probs = jnp.where(mask[None], jnp.exp(scores - log_total), 0.0)
    grad_prob = jnp.einsum(
        "qhd,kd->hqk", grad_out, keys[:, head_dim:], preferred_element_type=jnp.float32
    )
    delta = jnp.einsum("qhd,qhd->hq", grad_out.astype(jnp.float32), out)[:, :, None]
    grad_score = (probs * (grad_prob - delta)).astype(jnp.bfloat16)
    grad_query = jnp.einsum(
        "hqk,kd->qhd", grad_score, keys[:, :head_dim], preferred_element_type=jnp.float32
    )
    grad_key = jnp.einsum("hqk,qhd->kd", grad_score, query_s, preferred_element_type=jnp.float32)
    grad_value = jnp.einsum(
        "hqk,qhd->kd", probs.astype(jnp.bfloat16), grad_out, preferred_element_type=jnp.float32
    )
    return (grad_query, jnp.concatenate([grad_key, grad_value], -1))


def body(layer_input, w_qkv, w_out, w_gate_up, w_down, norm_gain, qk_gain, cotangent):
    wsh_count = lax.axis_size("wsh")
    seq_index = lax.axis_index("seq")
    wsh_index = lax.axis_index("wsh")
    rows = layer_input.shape[0]
    block = rows * wsh_count
    gathered = (
        lax.all_gather(w_qkv, "wsh", axis=0, tiled=True),
        lax.all_gather(w_out, "wsh", axis=0, tiled=True),
        lax.all_gather(w_gate_up, "wsh", axis=0, tiled=True),
        lax.all_gather(w_down, "wsh", axis=0, tiled=True),
        lax.all_gather(norm_gain, "wsh", axis=1, tiled=True),
        lax.all_gather(qk_gain, "wsh", axis=0, tiled=True),
    )
    qkv_full, out_full, gate_up_full, down_full, norm_full, qk_full = gathered
    gains = norm_full.astype(jnp.float32)
    head_dim = qk_full.shape[0] // 2
    heads = out_full.shape[1] // head_dim
    width_q = heads * head_dim
    hidden_units = down_full.shape[1]
    gain_query = qk_full[:head_dim].astype(jnp.float32)
    gain_key = qk_full[head_dim:].astype(jnp.float32)
    own_start = (seq_index * wsh_count + wsh_index) * rows
    positions = own_start + jnp.arange(rows, dtype=jnp.int32)
    key_pos = own_start - WIN + jnp.arange(WIN + rows, dtype=jnp.int32)
    mask = block_mask(positions, key_pos)
    cosine, sine = rope_tables(positions, head_dim)
    rows_f = layer_input.astype(jnp.float32)
    scale1 = inv_rms(rows_f)
    normed = (rows_f * scale1 * gains[0]).astype(jnp.bfloat16)
    projected = jnp.dot(normed, qkv_full, preferred_element_type=jnp.float32)
    query = projected[:, :width_q].reshape(rows, heads, head_dim)
    key = projected[:, width_q : width_q + head_dim]
    value = projected[:, width_q + head_dim :]
    scale_q = inv_rms(query)
    scale_k = inv_rms(key)
    query_s = (
        rotate(query * scale_q * gain_query, cosine[:, None], sine[:, None]) * head_dim ** (-0.5)
    ).astype(jnp.bfloat16)
    key_s = rotate(key * scale_k * gain_key, cosine, sine).astype(jnp.bfloat16)
    local_kv = jnp.concatenate([key_s, value.astype(jnp.bfloat16)], -1)
    block_kv = lax.all_gather(local_kv, "wsh", axis=0, tiled=True)
    previous = from_behind(block_kv, "seq", 1)
    keys = lax.dynamic_slice_in_dim(
        jnp.concatenate([previous, block_kv], 0), wsh_index * rows, WIN + rows, 0
    )
    attended, log_total = attend(query_s, keys, mask)
    attended_b = attended.reshape(rows, width_q).astype(jnp.bfloat16)
    branch = lax.dot_general(
        attended_b, out_full, (((1,), (1,)), ((), ())), preferred_element_type=jnp.float32
    )
    scale2 = inv_rms(branch)
    hidden_res = rows_f + branch * scale2 * gains[1]
    scale3 = inv_rms(hidden_res)
    ffn_in = (hidden_res * scale3 * gains[2]).astype(jnp.bfloat16)
    gate_up = jnp.dot(ffn_in, gate_up_full, preferred_element_type=jnp.float32)
    gate = gate_up[:, :hidden_units]
    upper = gate_up[:, hidden_units:]
    mixed = (gelu_tanh(gate) * upper).astype(jnp.bfloat16)
    ffn_out = lax.dot_general(
        mixed, down_full, (((1,), (1,)), ((), ())), preferred_element_type=jnp.float32
    )
    scale4 = inv_rms(ffn_out)
    output = (hidden_res + ffn_out * scale4 * gains[3]).astype(jnp.bfloat16)
    gathered = (
        lax.all_gather(w_qkv, "wsh", axis=0, tiled=True),
        lax.all_gather(w_out, "wsh", axis=0, tiled=True),
        lax.all_gather(w_gate_up, "wsh", axis=0, tiled=True),
        lax.all_gather(w_down, "wsh", axis=0, tiled=True),
        lax.all_gather(norm_gain, "wsh", axis=1, tiled=True),
        lax.all_gather(qk_gain, "wsh", axis=0, tiled=True),
    )
    qkv_full, out_full, gate_up_full, down_full, norm_full, qk_full = gathered
    gains = norm_full.astype(jnp.float32)
    gain_query = qk_full[:head_dim].astype(jnp.float32)
    gain_key = qk_full[head_dim:].astype(jnp.float32)
    grad_y = cotangent.astype(jnp.float32)
    grad_ffn, rows_three = norm_back(grad_y, ffn_out, scale4, gains[3])
    grad_ffn_b = grad_ffn.astype(jnp.bfloat16)
    grad_mixed = jnp.dot(grad_ffn_b, down_full, preferred_element_type=jnp.float32)
    grad_gu = jnp.concatenate(
        [grad_mixed * upper * gelu_slope(gate), grad_mixed * gelu_tanh(gate)], -1
    ).astype(jnp.bfloat16)
    grad_ffn_in = lax.dot_general(
        grad_gu, gate_up_full, (((1,), (1,)), ((), ())), preferred_element_type=jnp.float32
    )
    grad_res, rows_two = norm_back(grad_ffn_in, hidden_res, scale3, gains[2])
    grad_hidden = grad_y + grad_res
    grad_branch, rows_one = norm_back(grad_hidden, branch, scale2, gains[1])
    grad_branch_b = grad_branch.astype(jnp.bfloat16)
    grad_att = (
        jnp.dot(grad_branch_b, out_full, preferred_element_type=jnp.float32)
        .astype(jnp.bfloat16)
        .reshape(rows, heads, head_dim)
    )
    grad_query, grad_keys = attend_back(query_s, keys, mask, attended, log_total, grad_att)
    spread = lax.dynamic_update_slice_in_dim(
        jnp.zeros((WIN + block, 2 * head_dim), jnp.float32), grad_keys, wsh_index * rows, 0
    )
    returned = from_behind(spread[:WIN].astype(jnp.bfloat16), "seq", -1).astype(jnp.float32)
    own_part = spread[WIN:]
    own_part = jnp.concatenate([own_part[: block - WIN], own_part + returned], 0)
    grad_kv = lax.psum_scatter(
        own_part.astype(jnp.bfloat16), "wsh", scatter_dimension=0, tiled=True
    ).astype(jnp.float32)
    grad_qn = unrotate(grad_query, cosine[:, None], sine[:, None]) * head_dim ** (-0.5)
    grad_q, rows_query = norm_back(grad_qn, query, scale_q, gain_query)
    grad_kn = unrotate(grad_kv[:, :head_dim], cosine, sine)
    grad_k, rows_key = norm_back(grad_kn, key, scale_k, gain_key)
    grad_qkv = jnp.concatenate(
        [grad_q.reshape(rows, width_q), grad_k, grad_kv[:, head_dim:]], -1
    ).astype(jnp.bfloat16)
    grad_normed = lax.dot_general(
        grad_qkv, qkv_full, (((1,), (1,)), ((), ())), preferred_element_type=jnp.float32
    )
    grad_in, rows_zero = norm_back(grad_normed, rows_f, scale1, gains[0])
    grad_input = grad_hidden + grad_in
    gain_grads = jnp.stack(
        [jnp.sum(rows_zero, 0), jnp.sum(rows_one, 0), jnp.sum(rows_two, 0), jnp.sum(rows_three, 0)]
    )
    qk_grads = jnp.concatenate([jnp.sum(rows_query, (0, 1)), jnp.sum(rows_key, 0)], 0)
    terms = (
        outer_sum(normed, grad_qkv),
        outer_sum(grad_branch_b, attended_b),
        outer_sum(ffn_in, grad_gu),
        outer_sum(grad_ffn_b, mixed),
        gain_grads,
        qk_grads,
    )
    owned = (
        lax.psum_scatter(
            terms[0].astype(jnp.bfloat16), "wsh", scatter_dimension=0, tiled=True
        ).astype(jnp.float32),
        lax.psum_scatter(
            terms[1].astype(jnp.bfloat16), "wsh", scatter_dimension=0, tiled=True
        ).astype(jnp.float32),
        lax.psum_scatter(
            terms[2].astype(jnp.bfloat16), "wsh", scatter_dimension=0, tiled=True
        ).astype(jnp.float32),
        lax.psum_scatter(
            terms[3].astype(jnp.bfloat16), "wsh", scatter_dimension=0, tiled=True
        ).astype(jnp.float32),
        lax.psum_scatter(
            terms[4].astype(jnp.bfloat16), "wsh", scatter_dimension=1, tiled=True
        ).astype(jnp.float32),
        lax.psum_scatter(
            terms[5].astype(jnp.bfloat16), "wsh", scatter_dimension=0, tiled=True
        ).astype(jnp.float32),
    )
    grads = (
        lax.psum(owned[0].astype(jnp.bfloat16), "seq").astype(jnp.float32),
        lax.psum(owned[1].astype(jnp.bfloat16), "seq").astype(jnp.float32),
        lax.psum(owned[2].astype(jnp.bfloat16), "seq").astype(jnp.float32),
        lax.psum(owned[3].astype(jnp.bfloat16), "seq").astype(jnp.float32),
        lax.psum(owned[4].astype(jnp.bfloat16), "seq").astype(jnp.float32),
        lax.psum(owned[5].astype(jnp.bfloat16), "seq").astype(jnp.float32),
    )
    return (output, grad_input, grads[0], grads[1], grads[2], grads[3], grads[4], grads[5])


def solution(mesh):
    in_specs = (
        P(("seq", "wsh"), None),
        P("wsh", None),
        P("wsh", None),
        P("wsh", None),
        P("wsh", None),
        P(None, "wsh"),
        P("wsh"),
        P(("seq", "wsh"), None),
    )
    out_specs = (
        P(("seq", "wsh"), None),
        P(("seq", "wsh"), None),
        P("wsh", None),
        P("wsh", None),
        P("wsh", None),
        P("wsh", None),
        P(None, "wsh"),
        P("wsh"),
    )
    return jax.shard_map(body, mesh=mesh, in_specs=in_specs, out_specs=out_specs, check_vma=False)
```

profile of v0, /device:TPU:0, one launch (start us, length us, event | category | flops | bytes accessed | tf_op | source)
XLA Modules:
  0.0 865.7 jit_solution(17018947005329664847)
XLA Ops:
  10.1 6.2 all-gather
  16.4 5.3 all-gather.1
  22.6 20.4 %all-gather.7.cloned.1.call-done = bf16[1152,1536]{1,0:T(8,128)(2,1)} async-done(((bf16[288,1536]{1,0:T(8,128)(2,1)}), bf16[1152,1536]{1,0:T(8,128)(2,1)}) %all-gather.7.cloned.1.call-update) | async-done | bytes 3538960 | tf_op jit(solution)/shard_map/all_gather | solution.py:114
  43.0 2.7 fusion.50
  47.0 7.2 all_gather.30
  54.2 3.6 collective-permute-start
  58.4 10.9 %collective-permute-done = bf16[512,512]{1,0:T(8,128)(2,1)S(1)} collective-permute-done((bf16[512,512]{1,0:T(8,128)(2,1)S(1)}, bf16[512,512]{1,0:T(8,128)(2,1)S(1)}, u32[]{:S(2)}, u32[]{:S(2)}) %collective-permute-start) | collective-permute-done | bytes 524320 | tf_op jit(solution)/shard_map/ppermute | solution.py:14
  71.5 1.3 bitcast_convert_fusion
  72.8 2.7 multiply_reduce_fusion.6
  75.9 95.5 %all-gather.11.cloned.1.call-done = bf16[1152,6912]{1,0:T(8,128)(2,1)} async-done(((bf16[288,6912]{1,0:T(8,128)(2,1)}), bf16[1152,6912]{1,0:T(8,128)(2,1)}) %all-gather.11.cloned.1.call-update) | async-done | bytes 15925264 | tf_op jit(solution)/shard_map/all_gather | solution.py:116
  171.3 8.0 fusion.59
  179.4 1.8 copy-done
  181.8 46.8 %all-gather.13.cloned.1.call-done = bf16[1152,3456]{1,0:T(8,128)(2,1)} async-done(((bf16[288,3456]{1,0:T(8,128)(2,1)}), bf16[1152,3456]{1,0:T(8,128)(2,1)}) %all-gather.13.cloned.1.call-update) | async-done | bytes 7962640 | tf_op jit(solution)/shard_map/all_gather | solution.py:117
  228.6 6.0 multiply_reduce_fusion.4
  235.5 1.0 fusion.29
  236.4 3.4 fusion.6
  239.8 12.7 %multiply_reduce_fusion = (bf16[1152]{0:T(1024)(128)(2,1)}, f32[128]{0:T(128)S(1)}, f32[128,1152]{1,0:T(8,128)}) fusion(f32[128,1152]{1,0:T(8,128)S(1)} %get-tuple-element.33, f32[128]{0:T(128)S(1)} %add_rsqrt_fusion.2, f32[1152]{0:T(1024)S(1)} %get-tuple-element.21, bf16[1152,6912]{1,0:T(8,128)(2,1)} %all-gather.11.cloned.1.call-done, ...), kind=kOutput, calls=%fused_computation.67 | convolution fusion | flops 2042854144 | bytes 18882304 | tf_op jit(solution)/shard_map/dot_general | solution.py:190
  252.6 2.3 multiply_reduce_fusion.1
  258.2 1.2 copy.113
  259.5 1.9 convolution_bitcast_fusion.2
  261.4 1.1 fusion.41
  264.4 1.4 collective-permute-start.1
  265.9 14.7 %collective-permute-done.1 = bf16[512,512]{1,0:T(8,128)(2,1)S(1)} collective-permute-done((bf16[512,512]{1,0:T(8,128)(2,1)S(1)}, bf16[512,512]{1,0:T(8,128)(2,1)S(1)}, u32[]{:S(2)}, u32[]{:S(2)}) %collective-permute-start.1) | collective-permute-done | bytes 524320 | tf_op jit(solution)/shard_map/ppermute | solution.py:14
  280.5 1.0 fusion.13
  281.6 2.3 convolution_convert_fusion.3
  285.0 1.4 broadcast_multiply_fusion
  286.9 16.5 %reduce-scatter.9.cloned.1.call-done = bf16[128,512]{1,0:T(8,128)(2,1)} async-done(((bf16[512,512]{1,0:T(8,128)(2,1)}), bf16[128,512]{1,0:T(8,128)(2,1)}) %reduce-scatter.9.cloned.1.call-update) | async-done | bytes 131088 | tf_op jit(solution)/shard_map/reduce_scatter | solution.py:209
  305.2 1.1 multiply_reduce_fusion.10
  306.3 1.0 multiply_convert_fusion.5
  307.5 3.0 convolution_convert_fusion.2
  311.5 5.5 convolution_convert_fusion.1
  317.1 1.1 copy-done.7
  318.2 9.1 %convolution_convert_fusion = bf16[1152,6912]{1,0:T(8,128)(2,1)} fusion(bf16[128,3456]{1,0:T(8,128)(2,1)} %get-tuple-element.35, bf16[128,3456]{1,0:T(8,128)(2,1)S(1)} %copy-done.7, f32[128,1152]{1,0:T(8,128)S(1)} %get-tuple-element.33, f32[1152]{0:T(1024)S(1)} %get-tuple-element.21, f32[128]{0:T(128)S(1)} %copy-done.39), kind=kOutput, calls=%fused_computation | convolution fusion | flops 2050375680 | bytes 18289664 | tf_op jit(solution)/shard_map/dot_general | solution.py:69
  328.1 3.4 fusion.35
  332.5 6.1 reduce-scatter.13.cloned.1.call-done
  338.6 43.5 %reduce-scatter.11.cloned.1.call-done = bf16[288,1536]{1,0:T(8,128)(2,1)} async-done(((bf16[1152,1536]{1,0:T(8,128)(2,1)}), bf16[288,1536]{1,0:T(8,128)(2,1)}) %reduce-scatter.11.cloned.1.call-update) | async-done | bytes 884752 | tf_op jit(solution)/shard_map/reduce_scatter | solution.py:237
  382.1 72.1 %reduce-scatter.17.cloned.1.call-done = bf16[288,3456]{1,0:T(8,128)(2,1)} async-done(((bf16[1152,3456]{1,0:T(8,128)(2,1)}), bf16[288,3456]{1,0:T(8,128)(2,1)}) %reduce-scatter.17.cloned.1.call-update) | async-done | bytes 1990672 | tf_op jit(solution)/shard_map/reduce_scatter | solution.py:246
  454.2 122.7 %reduce-scatter.15.cloned.1.call-done = bf16[288,6912]{1,0:T(8,128)(2,1)} async-done(((bf16[1152,6912]{1,0:T(8,128)(2,1)}), bf16[288,6912]{1,0:T(8,128)(2,1)}) %reduce-scatter.15.cloned.1.call-update) | async-done | bytes 3981328 | tf_op jit(solution)/shard_map/reduce_scatter | solution.py:243
  578.8 5.8 all-reduce
  584.6 1.0 fusion.34
  585.7 14.4 %reduce-scatter.19.cloned.1.call-done = bf16[288,4]{1,0:T(8,128)(2,1)} async-done(((bf16[1152,4]{1,0:T(8,128)(2,1)}), bf16[288,4]{1,0:T(8,128)(2,1)}) %reduce-scatter.19.cloned.1.call-update) | async-done | bytes 2320
  600.0 1.0 copy.125
  601.0 22.0 %all-reduce.1 = (bf16[4,288]{1,0:T(4,128)(2,1)S(1)}, bf16[128]{0:T(256)(128)(2,1)S(1)}) all-reduce(bf16[4,288]{1,0:T(4,128)(2,1)S(1)} %copy.125, bf16[128]{0:T(256)(128)(2,1)S(1)} %dynamic-slice.1), channel_id=1, replica_groups=mesh['seq'=8,'wsh'=4] {'seq'}, use_global_device_ids=true, to_apply=%region_27.28 | all-reduce | flops 1280 | bytes 5120 | tf_op jit(solution)/shard_map/psum | solution.py:261
  624.1 224.1 %all-reduce.5.cloned.1.call-done = (bf16[288,1536]{1,0:T(8,128)(2,1)}, bf16[288,1024]{1,0:T(8,128)(2,1)}, bf16[288,6912]{1,0:T(8,128)(2,1)}, bf16[288,3456]{1,0:T(8,128)(2,1)}) async-done(((bf16[288,1536]{1,0:T(8,128)(2,1)}, bf16[288,1024]{1,0:T(8,128)(2,1)}, bf16[288,6912]{1,0:T(8,128)(2,1)}, bf16[288,3456]{1,0:T(8,128)(2,1)}), (bf16[288,1536]{1,0:T(8,128)(2,1)}, bf16[288,1024]{1,0:T(8,128)(2,1)}, ...) | async-done | bytes 7446544 | tf_op jit(solution)/shard_map/psum | solution.py:257
  848.3 2.7 convert_element_type.146
  851.0 2.2 convert_element_type.148
  853.2 3.8 convert_element_type.150
  857.0 2.2 convert_element_type.152
  (199 shorter events, 23.2 us)
Async XLA Ops:
  7.2 35.9 %all-gather.7.cloned.1.call-start = ((), (), s32[]{:S(2)}) async-start(), calls=%async_computation.6 | async-start | bytes 4423680 | tf_op jit(solution)/shard_map/all_gather | solution.py:114
  7.9 64.9 %all-gather.9.cloned.1.call-start = ((), (), s32[]{:S(2)}) async-start(), calls=%async_computation.7 | async-start | bytes 2949120 | tf_op jit(solution)/shard_map/all_gather | solution.py:115
  8.7 162.7 %all-gather.11.cloned.1.call-start = ((), (), s32[]{:S(2)}) async-start(), calls=%async_computation.8 | async-start | bytes 19906560 | tf_op jit(solution)/shard_map/all_gather | solution.py:116
  9.4 7.0 copy-start.49
  9.4 12.4 %copy-start.4 = (bf16[128,1152]{1,0:T(8,128)(2,1)S(1)}, bf16[128,1152]{1,0:T(8,128)(2,1)}, u32[]{:S(2)}) copy-start(bf16[128,1152]{1,0:T(8,128)(2,1)} %param.8) | copy-start | bytes 884740
  9.4 219.2 %all-gather.13.cloned.1.call-start = ((), (), s32[]{:S(2)}) async-start(), calls=%async_computation.9 | async-start | bytes 9953280 | tf_op jit(solution)/shard_map/all_gather | solution.py:117
  10.0 293.4 %reduce-scatter.9.cloned.1.call-start = ((), (), s32[]{:S(2)}) async-start(), calls=%async_computation.10 | async-start | bytes 655360 | tf_op jit(solution)/shard_map/reduce_scatter | solution.py:209
  22.0 23.8 %copy-start.46 = (f32[128]{0:T(128)}, f32[128]{0:T(128)S(1)}, u32[]{:S(2)}) copy-start(f32[128]{0:T(128)S(1)} %add_rsqrt_fusion.5) | copy-start | bytes 1540
  22.0 24.9 %copy-start.36 = (f32[2,1,128]{2,1,0:T(1,128)}, f32[2,1,128]{2,1,0:T(1,128)S(1)}, u32[]{:S(2)}) copy-start(f32[2,1,128]{2,1,0:T(1,128)S(1)} %get-tuple-element.49) | copy-start | bytes 3076
  22.0 36.2 %copy-start.43 = (f32[2,1,128]{2,1,0:T(1,128)}, f32[2,1,128]{2,1,0:T(1,128)S(1)}, u32[]{:S(2)}) copy-start(f32[2,1,128]{2,1,0:T(1,128)S(1)} %get-tuple-element.50) | copy-start | bytes 3076
  22.2 48.3 %copy-start.32 = (pred[128,640]{0,1:T(8,128)(4,1)}, pred[128,640]{0,1:T(8,128)(4,1)S(1)}, u32[]{:S(2)}) copy-start(pred[128,640]{0,1:T(8,128)(4,1)S(1)} %fusion.43) | copy-start | bytes 245764
  22.6 24.3 %copy-start.23 = (f32[128,128]{1,0:T(8,128)}, f32[128,128]{1,0:T(8,128)S(1)}, u32[]{:S(2)}) copy-start(f32[128,128]{1,0:T(8,128)S(1)} %get-tuple-element.51) | copy-start | bytes 196612
  22.6 24.3 %copy-start.30 = (f32[128,128]{1,0:T(8,128)}, f32[128,128]{1,0:T(8,128)S(1)}, u32[]{:S(2)}) copy-start(f32[128,128]{1,0:T(8,128)S(1)} %get-tuple-element.52) | copy-start | bytes 196612
  46.7 11.4 %copy-start.44 = (f32[128]{0:T(128)}, f32[128]{0:T(128)S(1)}, u32[]{:S(2)}) copy-start(f32[128]{0:T(128)S(1)} %add_rsqrt_fusion.4) | copy-start | bytes 1540
  54.2 15.0 %collective-permute-start = (bf16[512,512]{1,0:T(8,128)(2,1)S(1)}, bf16[512,512]{1,0:T(8,128)(2,1)S(1)}, u32[]{:S(2)}, u32[]{:S(2)}) collective-permute-start(bf16[512,512]{1,0:T(8,128)(2,1)S(1)} %all_gather.30), channel_id=1, source_target_pairs={{0,4},{4,8},{8,12},{12,16},{16,20},{20,24},{24,28},{1,5},{5,9},{9,... | collective-permute-start | bytes 1572872 | tf_op jit(solution)/shard_map/ppermute | solution.py:14
  58.0 12.1 %copy-start.22 = (f32[128,256]{0,1:T(8,128)}, f32[128,256]{0,1:T(8,128)S(1)}, u32[]{:S(2)}) copy-start(f32[128,256]{0,1:T(8,128)S(1)} %copy.91) | copy-start | bytes 393220
  58.1 11.9 %copy-start.20 = (f32[128,256]{0,1:T(8,128)}, f32[128,256]{0,1:T(8,128)S(1)}, u32[]{:S(2)}) copy-start(f32[128,256]{0,1:T(8,128)S(1)} %copy.90) | copy-start | bytes 393220
  58.4 12.1 %copy-start.27 = (bf16[128,4,256]{0,2,1:T(8,128)(2,1)}, bf16[128,4,256]{0,2,1:T(8,128)(2,1)S(1)}, u32[]{:S(2)}) copy-start(bf16[128,4,256]{0,2,1:T(8,128)(2,1)S(1)} %fusion.40) | copy-start | bytes 786436
  72.8 3.0 copy-start.25
  75.9 176.7 %copy-start.38 = (f32[128]{0:T(128)}, f32[128]{0:T(128)S(1)}, u32[]{:S(2)}) copy-start(f32[128]{0:T(128)S(1)} %add_rsqrt_fusion.2) | copy-start | bytes 1540
  179.4 1.8 copy-start
  181.8 52.8 %copy-start.8 = (bf16[128,1152]{1,0:T(8,128)(2,1)S(1)}, bf16[128,1152]{1,0:T(8,128)(2,1)}, u32[]{:S(2)}) copy-start(bf16[128,1152]{1,0:T(8,128)(2,1)} %param.15) | copy-start | bytes 884740
  228.6 7.8 copy-start.1
  228.6 7.8 copy-start.3
  236.4 3.4 copy-start.14
  252.6 3.2 copy-start.2
  256.3 3.2 copy-start.33
  259.5 3.1 copy-start.17
  259.5 3.1 copy-start.19
  259.5 3.1 copy-start.29
  264.3 17.3 %copy-start.10 = (bf16[128,1152]{1,0:T(8,128)(2,1)S(1)}, bf16[128,1152]{1,0:T(8,128)(2,1)}, u32[]{:S(2)}) copy-start(bf16[128,1152]{1,0:T(8,128)(2,1)} %copy-done.9) | copy-start | bytes 884740
  264.4 17.3 %copy-start.26 = (bf16[128,4,256]{0,2,1:T(8,128)(2,1)S(1)}, bf16[128,4,256]{0,2,1:T(8,128)(2,1)}, u32[]{:S(2)}) copy-start(bf16[128,4,256]{0,2,1:T(8,128)(2,1)} %copy-done.25) | copy-start | bytes 786436
  264.4 16.1 %collective-permute-start.1 = (bf16[512,512]{1,0:T(8,128)(2,1)S(1)}, bf16[512,512]{1,0:T(8,128)(2,1)S(1)}, u32[]{:S(2)}, u32[]{:S(2)}) collective-permute-start(bf16[512,512]{1,0:T(8,128)(2,1)S(1)} %slice.205), channel_id=1, source_target_pairs={{4,0},{8,4},{12,8},{16,12},{20,16},{24,20},{28,24},{5,1},{9,5},{13... | collective-permute-start | bytes 1572872 | tf_op jit(solution)/shard_map/ppermute | solution.py:14
  281.5 57.0 %reduce-scatter.13.cloned.1.call-start = ((), (), s32[]{:S(2)}) async-start(), calls=%async_computation.12 | async-start | bytes 2949120 | tf_op jit(solution)/shard_map/reduce_scatter | solution.py:240
  283.9 98.2 %reduce-scatter.11.cloned.1.call-start = ((), (), s32[]{:S(2)}) async-start(), calls=%async_computation.11 | async-start | bytes 4423680 | tf_op jit(solution)/shard_map/reduce_scatter | solution.py:237
  284.0 2.5 copy-start.21
  284.0 2.5 copy-start.35
  286.5 17.9 %copy-start.31 = (f32[128,128]{1,0:T(8,128)S(1)}, f32[128,128]{1,0:T(8,128)}, u32[]{:S(2)}) copy-start(f32[128,128]{1,0:T(8,128)} %copy-done.30) | copy-start | bytes 196612
  286.5 18.7 %copy-start.24 = (f32[128,128]{1,0:T(8,128)S(1)}, f32[128,128]{1,0:T(8,128)}, u32[]{:S(2)}) copy-start(f32[128,128]{1,0:T(8,128)} %copy-done.23) | copy-start | bytes 196612
  286.5 18.7 %copy-start.37 = (f32[2,1,128]{2,1,0:T(1,128)S(1)}, f32[2,1,128]{2,1,0:T(1,128)}, u32[]{:S(2)}) copy-start(f32[2,1,128]{2,1,0:T(1,128)} %copy-done.36) | copy-start | bytes 3076
  286.5 18.7 %copy-start.45 = (f32[128]{0:T(128)S(1)}, f32[128]{0:T(128)}, u32[]{:S(2)}) copy-start(f32[128]{0:T(128)} %copy-done.44) | copy-start | bytes 1540
  286.7 20.8 %copy-start.47 = (f32[128]{0:T(128)S(1)}, f32[128]{0:T(128)}, u32[]{:S(2)}) copy-start(f32[128]{0:T(128)} %copy-done.46) | copy-start | bytes 1540
  310.5 143.7 %reduce-scatter.17.cloned.1.call-start = ((), (), s32[]{:S(2)}) async-start(), calls=%async_computation.14 | async-start | bytes 9953280 | tf_op jit(solution)/shard_map/reduce_scatter | solution.py:246
  317.0 259.8 %reduce-scatter.15.cloned.1.call-start = ((), (), s32[]{:S(2)}) async-start(), calls=%async_computation.13 | async-start | bytes 19906560 | tf_op jit(solution)/shard_map/reduce_scatter | solution.py:243
  327.4 272.6 %reduce-scatter.19.cloned.1.call-start = ((), (), s32[]{:S(2)}) async-start(), calls=%async_computation.15 | async-start | bytes 368640
  332.5 515.8 %all-reduce.5.cloned.1.call-start = ((), (), s32[]{:S(2)}) async-start(), calls=%async_computation.16 | async-start | bytes 14893056 | tf_op jit(solution)/shard_map/psum | solution.py:257
  848.3 4.9 copy-start.6
  853.2 3.8 copy-start.13
  (16 other events, 14.7 us)
Sparse Core Ops, SparseCore 0:
  9.5 33.4 all-gather.6
  44.6 24.0 all-gather.8
  70.2 101.0 all-gather.10
  172.7 55.8 all-gather.12
  281.7 21.6 reduce-scatter.8
  305.7 32.7 reduce-scatter.12
  341.7 40.3 reduce-scatter.10
  385.3 68.8 reduce-scatter.16
  456.8 120.0 reduce-scatter.14
  579.8 20.2 reduce-scatter.18
  604.6 243.6 all-reduce.4
where the time goes:
time: 867 us; the launch traced here: 866 us
  waiting for transfers between devices  690 us (80%)
  matrix products  65.2 us (8%)
  blocking collectives  46.5 us (5%)
  other arithmetic  27.9 us (3%)
  between operations  15.5 us (2%)
  local copies, waits for them, and re-layouts  15 us (2%)
    psum x1, waiting for transfers between devices, body(): lax.psum(owned[0].astype(jnp.bfloat16), 'seq').astype(jnp.float32)  224 us
    reduce_scatter x1, waiting for transfers between devices, body(): lax.psum_scatter(terms[2].astype(jnp.bfloat16), 'wsh', scatter_dimension=...  123 us
    all_gather x1, waiting for transfers between devices, body(): lax.all_gather(w_gate_up, 'wsh', axis=0, tiled=True)  95.5 us
    reduce_scatter x1, waiting for transfers between devices, body(): lax.psum_scatter(terms[3].astype(jnp.bfloat16), 'wsh', scatter_dimension=...  72.1 us
    all_gather x1, waiting for transfers between devices, body(): lax.all_gather(w_down, 'wsh', axis=0, tiled=True)  46.8 us
    reduce_scatter x1, waiting for transfers between devices, body(): lax.psum_scatter(terms[0].astype(jnp.bfloat16), 'wsh', scatter_dimension=...  43.5 us
    ppermute x2, waiting for transfers between devices, from_behind(): return lax.ppermute(value, axis, pairs)  25.5 us
    psum x1, blocking collectives, body(): lax.psum(owned[4].astype(jnp.bfloat16), 'seq').astype(jnp.float32)  22 us
  transfers between devices with their start and end apart: 13, of which 12 were waited for; matrix products, arithmetic and copies ran while one was open for 6% of the time, Pallas kernels for 0%

commit v1 on v0

--- a/solution.py
+++ b/solution.py
@@ -254,7 +254,7 @@
         ).astype(jnp.float32),
     )
     grads = (
-        lax.psum(owned[0].astype(jnp.bfloat16), "seq").astype(jnp.float32),
+        jnp.sum(lax.all_gather(owned[0].astype(jnp.bfloat16), "seq"), axis=0).astype(jnp.float32),
         lax.psum(owned[1].astype(jnp.bfloat16), "seq").astype(jnp.float32),
         lax.psum(owned[2].astype(jnp.bfloat16), "seq").astype(jnp.float32),
         lax.psum(owned[3].astype(jnp.bfloat16), "seq").astype(jnp.float32),

time: 867 us -> 955 us (1.10)
  waiting for transfers between devices: 690 us -> 770 us
    all_gather x0 -> x1, waiting for transfers between devices: none -> 86.4 us  [body(): lax.all_gather(owned[0].astype(jnp.bfloat16), 'seq')]
    reduce_scatter x1, waiting for transfers between devices: 6.06 us -> 35.3 us  [body(): lax.psum_scatter(terms[1].astype(jnp.bfloat16), 'wsh', scatter_dimension=...]
    reduce_scatter x1, waiting for transfers between devices: 43.5 us -> 15.4 us  [body(): lax.psum_scatter(terms[0].astype(jnp.bfloat16), 'wsh', scatter_dimension=...]
  transfers between devices with their start and end apart: 13 -> 14, of which waited for: 12 -> 13; matrix products, arithmetic and copies ran while one was open for 6% -> 6% of each run, Pallas kernels for 0% -> 0%
where the time goes in v1:
time: 955 us; the launch traced here: 954 us
  waiting for transfers between devices  770 us (81%)
  matrix products  65.3 us (7%)
  blocking collectives  46.6 us (5%)
  other arithmetic  34.3 us (4%)
  between operations  15.9 us (2%)
  local copies, waits for them, and re-layouts  15.7 us (2%)
    psum x1, waiting for transfers between devices, body(): lax.psum(owned[1].astype(jnp.bfloat16), 'seq').astype(jnp.float32)  215 us
    reduce_scatter x1, waiting for transfers between devices, body(): lax.psum_scatter(terms[2].astype(jnp.bfloat16), 'wsh', scatter_dimension=...  123 us
    all_gather x1, waiting for transfers between devices, body(): lax.all_gather(w_gate_up, 'wsh', axis=0, tiled=True)  95.5 us
    all_gather x1, waiting for transfers between devices, body(): lax.all_gather(owned[0].astype(jnp.bfloat16), 'seq')  86.4 us
    reduce_scatter x1, waiting for transfers between devices, body(): lax.psum_scatter(terms[3].astype(jnp.bfloat16), 'wsh', scatter_dimension=...  72 us
    all_gather x1, waiting for transfers between devices, body(): lax.all_gather(w_down, 'wsh', axis=0, tiled=True)  46.8 us
    reduce_scatter x1, waiting for transfers between devices, body(): lax.psum_scatter(terms[1].astype(jnp.bfloat16), 'wsh', scatter_dimension=...  35.3 us
    ppermute x2, waiting for transfers between devices, from_behind(): return lax.ppermute(value, axis, pairs)  24.5 us
  transfers between devices with their start and end apart: 14, of which 13 were waited for; matrix products, arithmetic and copies ran while one was open for 6% of the time, Pallas kernels for 0%

profile of v1, /device:TPU:0, one launch (start us, length us, event | category | flops | bytes accessed | tf_op | source)
XLA Modules:
  0.0 953.8 jit_solution(15511145356568637675)
XLA Ops:
  10.1 6.2 all-gather.1
  16.4 5.3 all-gather.2
  22.6 20.4 %all-gather.9.cloned.1.call-done = bf16[1152,1536]{1,0:T(8,128)(2,1)} async-done(((bf16[288,1536]{1,0:T(8,128)(2,1)}), bf16[1152,1536]{1,0:T(8,128)(2,1)}) %all-gather.9.cloned.1.call-update) | async-done | bytes 3538960 | tf_op jit(solution)/shard_map/all_gather | solution.py:114
  43.0 2.7 fusion.50
  47.0 7.2 all_gather.36
  54.2 3.6 collective-permute-start
  58.8 10.5 %collective-permute-done = bf16[512,512]{1,0:T(8,128)(2,1)S(1)} collective-permute-done((bf16[512,512]{1,0:T(8,128)(2,1)S(1)}, bf16[512,512]{1,0:T(8,128)(2,1)S(1)}, u32[]{:S(2)}, u32[]{:S(2)}) %collective-permute-start) | collective-permute-done | bytes 524320 | tf_op jit(solution)/shard_map/ppermute | solution.py:14
  70.5 1.0 copy-done.16
  71.5 1.3 bitcast_convert_fusion
  72.8 2.7 multiply_reduce_fusion.6
  75.9 95.5 %all-gather.13.cloned.1.call-done = bf16[1152,6912]{1,0:T(8,128)(2,1)} async-done(((bf16[288,6912]{1,0:T(8,128)(2,1)}), bf16[1152,6912]{1,0:T(8,128)(2,1)}) %all-gather.13.cloned.1.call-update) | async-done | bytes 15925264 | tf_op jit(solution)/shard_map/all_gather | solution.py:116
  171.3 8.1 fusion.59
  179.4 1.8 copy-done
  181.8 46.8 %all-gather.15.cloned.1.call-done = bf16[1152,3456]{1,0:T(8,128)(2,1)} async-done(((bf16[288,3456]{1,0:T(8,128)(2,1)}), bf16[1152,3456]{1,0:T(8,128)(2,1)}) %all-gather.15.cloned.1.call-update) | async-done | bytes 7962640 | tf_op jit(solution)/shard_map/all_gather | solution.py:117
  228.6 6.0 multiply_reduce_fusion.4
  236.4 3.4 fusion.6
  239.8 12.7 %multiply_reduce_fusion = (bf16[1152]{0:T(1024)(128)(2,1)}, f32[128]{0:T(128)S(1)}, f32[128,1152]{1,0:T(8,128)}) fusion(f32[128,1152]{1,0:T(8,128)S(1)} %get-tuple-element.32, f32[128]{0:T(128)S(1)} %add_rsqrt_fusion.2, f32[1152]{0:T(1024)S(1)} %get-tuple-element.21, bf16[1152,6912]{1,0:T(8,128)(2,1)} %all-gather.13.cloned.1.call-done, ...), kind=kOutput, calls=%fused_computation.67 | convolution fusion | flops 2042854144 | bytes 18882304 | tf_op jit(solution)/shard_map/dot_general | solution.py:190
  252.6 2.3 multiply_reduce_fusion.1
  258.2 1.2 copy.113
  259.5 1.9 convolution_bitcast_fusion.2
  261.4 1.1 fusion.41
  262.6 1.1 fusion.9
  264.7 1.3 collective-permute-start.1
  266.5 14.1 %collective-permute-done.1 = bf16[512,512]{1,0:T(8,128)(2,1)S(1)} collective-permute-done((bf16[512,512]{1,0:T(8,128)(2,1)S(1)}, bf16[512,512]{1,0:T(8,128)(2,1)S(1)}, u32[]{:S(2)}, u32[]{:S(2)}) %collective-permute-start.1) | collective-permute-done | bytes 524320 | tf_op jit(solution)/shard_map/ppermute | solution.py:14
  281.7 1.4 broadcast_multiply_fusion
  284.2 19.2 %reduce-scatter.9.cloned.1.call-done = bf16[128,512]{1,0:T(8,128)(2,1)} async-done(((bf16[512,512]{1,0:T(8,128)(2,1)}), bf16[128,512]{1,0:T(8,128)(2,1)}) %reduce-scatter.9.cloned.1.call-update) | async-done | bytes 131088 | tf_op jit(solution)/shard_map/reduce_scatter | solution.py:209
  305.4 1.6 multiply_reduce_fusion.10
  308.1 3.0 convolution_convert_fusion.2
  312.2 2.2 convolution_convert_fusion.3
  315.3 6.0 convolution_convert_fusion.1
  321.5 1.1 copy-done.6
  322.9 8.1 convolution_convert_fusion
  331.9 3.4 fusion.35
  336.3 15.4 %reduce-scatter.11.cloned.1.call-done = bf16[288,1536]{1,0:T(8,128)(2,1)} async-done(((bf16[1152,1536]{1,0:T(8,128)(2,1)}), bf16[288,1536]{1,0:T(8,128)(2,1)}) %reduce-scatter.11.cloned.1.call-update) | async-done | bytes 884752 | tf_op jit(solution)/shard_map/reduce_scatter | solution.py:237
  351.7 35.3 %reduce-scatter.13.cloned.1.call-done = bf16[288,1024]{1,0:T(8,128)(2,1)} async-done(((bf16[1152,1024]{1,0:T(8,128)(2,1)}), bf16[288,1024]{1,0:T(8,128)(2,1)}) %reduce-scatter.13.cloned.1.call-update) | async-done | bytes 589840 | tf_op jit(solution)/shard_map/reduce_scatter | solution.py:240
  387.1 72.0 %reduce-scatter.17.cloned.1.call-done = bf16[288,3456]{1,0:T(8,128)(2,1)} async-done(((bf16[1152,3456]{1,0:T(8,128)(2,1)}), bf16[288,3456]{1,0:T(8,128)(2,1)}) %reduce-scatter.17.cloned.1.call-update) | async-done | bytes 1990672 | tf_op jit(solution)/shard_map/reduce_scatter | solution.py:246
  459.1 122.7 %reduce-scatter.15.cloned.1.call-done = bf16[288,6912]{1,0:T(8,128)(2,1)} async-done(((bf16[1152,6912]{1,0:T(8,128)(2,1)}), bf16[288,6912]{1,0:T(8,128)(2,1)}) %reduce-scatter.15.cloned.1.call-update) | async-done | bytes 3981328 | tf_op jit(solution)/shard_map/reduce_scatter | solution.py:243
  583.7 5.8 all-reduce
  589.6 1.0 fusion.34
  590.6 14.3 %reduce-scatter.19.cloned.1.call-done = bf16[288,4]{1,0:T(8,128)(2,1)} async-done(((bf16[1152,4]{1,0:T(8,128)(2,1)}), bf16[288,4]{1,0:T(8,128)(2,1)}) %reduce-scatter.19.cloned.1.call-update) | async-done | bytes 2320
  605.9 22.1 %all-reduce.1 = (bf16[4,288]{1,0:T(4,128)(2,1)S(1)}, bf16[128]{0:T(256)(128)(2,1)S(1)}) all-reduce(bf16[4,288]{1,0:T(4,128)(2,1)S(1)} %copy.125, bf16[128]{0:T(256)(128)(2,1)S(1)} %dynamic-slice.1), channel_id=1, replica_groups=mesh['seq'=8,'wsh'=4] {'seq'}, use_global_device_ids=true, to_apply=%region_27.28 | all-reduce | flops 1280 | bytes 5120 | tf_op jit(solution)/shard_map/psum | solution.py:261
  629.2 86.4 %all-gather.17.cloned.1.call-done = bf16[2304,1536]{1,0:T(8,128)(2,1)} async-done(((bf16[288,1536]{1,0:T(8,128)(2,1)}), bf16[2304,1536]{1,0:T(8,128)(2,1)}) %all-gather.17.cloned.1.call-update) | async-done | bytes 7077904 | tf_op jit(solution)/shard_map/all_gather | solution.py:257
  715.6 4.5 reduce_sum.196
  720.1 1.4 convert_element_type.148
  721.5 215.0 %all-reduce.5.cloned.1.call-done = (bf16[288,1024]{1,0:T(8,128)(2,1)}, bf16[288,6912]{1,0:T(8,128)(2,1)}, bf16[288,3456]{1,0:T(8,128)(2,1)}) async-done(((bf16[288,1024]{1,0:T(8,128)(2,1)}, bf16[288,6912]{1,0:T(8,128)(2,1)}, bf16[288,3456]{1,0:T(8,128)(2,1)}), (bf16[288,1024]{1,0:T(8,128)(2,1)}, bf16[288,6912]{1,0:T(8,128)(2,1)}, bf16[288,3456]{1,0:T(8,128)(2,1)})) %all-reduce.5.cloned.1.call-update) | async-done | bytes 6561808 | tf_op jit(solution)/shard_map/psum | solution.py:258
  936.5 2.2 convert_element_type.150
  938.7 6.0 convert_element_type.152
  944.7 2.2 convert_element_type.154
  (221 shorter events, 27.1 us)
Async XLA Ops:
  7.2 35.9 %all-gather.9.cloned.1.call-start = ((), (), s32[]{:S(2)}) async-start(), calls=%async_computation.6 | async-start | bytes 4423680 | tf_op jit(solution)/shard_map/all_gather | solution.py:114
  7.9 64.9 %all-gather.11.cloned.1.call-start = ((), (), s32[]{:S(2)}) async-start(), calls=%async_computation.7 | async-start | bytes 2949120 | tf_op jit(solution)/shard_map/all_gather | solution.py:115
  8.7 162.7 %all-gather.13.cloned.1.call-start = ((), (), s32[]{:S(2)}) async-start(), calls=%async_computation.8 | async-start | bytes 19906560 | tf_op jit(solution)/shard_map/all_gather | solution.py:116
  9.4 7.0 copy-start.58
  9.4 12.4 %copy-start.4 = (bf16[128,1152]{1,0:T(8,128)(2,1)S(1)}, bf16[128,1152]{1,0:T(8,128)(2,1)}, u32[]{:S(2)}) copy-start(bf16[128,1152]{1,0:T(8,128)(2,1)} %param.8) | copy-start | bytes 884740
  9.4 219.2 %all-gather.15.cloned.1.call-start = ((), (), s32[]{:S(2)}) async-start(), calls=%async_computation.9 | async-start | bytes 9953280 | tf_op jit(solution)/shard_map/all_gather | solution.py:117
  10.0 293.5 %reduce-scatter.9.cloned.1.call-start = ((), (), s32[]{:S(2)}) async-start(), calls=%async_computation.10 | async-start | bytes 655360 | tf_op jit(solution)/shard_map/reduce_scatter | solution.py:209
  22.0 23.8 %copy-start.52 = (f32[128]{0:T(128)}, f32[128]{0:T(128)S(1)}, u32[]{:S(2)}) copy-start(f32[128]{0:T(128)S(1)} %add_rsqrt_fusion.5) | copy-start | bytes 1540
  22.0 24.9 %copy-start.39 = (f32[2,1,128]{2,1,0:T(1,128)}, f32[2,1,128]{2,1,0:T(1,128)S(1)}, u32[]{:S(2)}) copy-start(f32[2,1,128]{2,1,0:T(1,128)S(1)} %get-tuple-element.48) | copy-start | bytes 3076
  22.0 36.2 %copy-start.46 = (f32[2,1,128]{2,1,0:T(1,128)}, f32[2,1,128]{2,1,0:T(1,128)S(1)}, u32[]{:S(2)}) copy-start(f32[2,1,128]{2,1,0:T(1,128)S(1)} %get-tuple-element.49) | copy-start | bytes 3076
  22.2 48.3 %copy-start.30 = (pred[128,640]{0,1:T(8,128)(4,1)}, pred[128,640]{0,1:T(8,128)(4,1)S(1)}, u32[]{:S(2)}) copy-start(pred[128,640]{0,1:T(8,128)(4,1)S(1)} %fusion.43) | copy-start | bytes 245764
  22.6 24.3 %copy-start.21 = (f32[128,128]{1,0:T(8,128)}, f32[128,128]{1,0:T(8,128)S(1)}, u32[]{:S(2)}) copy-start(f32[128,128]{1,0:T(8,128)S(1)} %get-tuple-element.50) | copy-start | bytes 196612
  22.6 24.3 %copy-start.28 = (f32[128,128]{1,0:T(8,128)}, f32[128,128]{1,0:T(8,128)S(1)}, u32[]{:S(2)}) copy-start(f32[128,128]{1,0:T(8,128)S(1)} %get-tuple-element.51) | copy-start | bytes 196612
  46.7 11.4 %copy-start.49 = (f32[128]{0:T(128)}, f32[128]{0:T(128)S(1)}, u32[]{:S(2)}) copy-start(f32[128]{0:T(128)S(1)} %add_rsqrt_fusion.4) | copy-start | bytes 1540
  54.2 15.0 %collective-permute-start = (bf16[512,512]{1,0:T(8,128)(2,1)S(1)}, bf16[512,512]{1,0:T(8,128)(2,1)S(1)}, u32[]{:S(2)}, u32[]{:S(2)}) collective-permute-start(bf16[512,512]{1,0:T(8,128)(2,1)S(1)} %all_gather.36), channel_id=1, source_target_pairs={{0,4},{4,8},{8,12},{12,16},{16,20},{20,24},{24,28},{1,5},{5,9},{9,... | collective-permute-start | bytes 1572872 | tf_op jit(solution)/shard_map/ppermute | solution.py:14
  58.0 12.1 %copy-start.20 = (f32[128,256]{0,1:T(8,128)}, f32[128,256]{0,1:T(8,128)S(1)}, u32[]{:S(2)}) copy-start(f32[128,256]{0,1:T(8,128)S(1)} %copy.91) | copy-start | bytes 393220
  58.8 11.7 %copy-start.25 = (bf16[128,4,256]{0,2,1:T(8,128)(2,1)}, bf16[128,4,256]{0,2,1:T(8,128)(2,1)S(1)}, u32[]{:S(2)}) copy-start(bf16[128,4,256]{0,2,1:T(8,128)(2,1)S(1)} %fusion.40) | copy-start | bytes 786436
  70.1 2.7 copy-start.14
  70.5 189.0 %copy-start.51 = (f32[4,128]{1,0:T(4,128)}, f32[4,128]{1,0:T(4,128)S(1)}, u32[]{:S(2)}) copy-start(f32[4,128]{1,0:T(4,128)S(1)} %log.8) | copy-start | bytes 6148
  72.8 3.0 copy-start.23
  75.8 176.7 %copy-start.41 = (f32[128]{0:T(128)}, f32[128]{0:T(128)S(1)}, u32[]{:S(2)}) copy-start(f32[128]{0:T(128)S(1)} %add_rsqrt_fusion.2) | copy-start | bytes 1540
  181.8 52.8 %copy-start.8 = (bf16[128,1152]{1,0:T(8,128)(2,1)S(1)}, bf16[128,1152]{1,0:T(8,128)(2,1)}, u32[]{:S(2)}) copy-start(bf16[128,1152]{1,0:T(8,128)(2,1)} %param.15) | copy-start | bytes 884740
  228.6 7.8 copy-start.1
  228.6 7.8 copy-start.3
  236.4 3.4 copy-start.12
  252.6 3.2 copy-start.2
  256.3 3.2 copy-start.31
  259.5 3.1 copy-start.15
  259.5 3.1 copy-start.17
  259.5 3.1 copy-start.27
  259.5 3.1 copy-start.32
  264.7 16.0 %collective-permute-start.1 = (bf16[512,512]{1,0:T(8,128)(2,1)S(1)}, bf16[512,512]{1,0:T(8,128)(2,1)S(1)}, u32[]{:S(2)}, u32[]{:S(2)}) collective-permute-start(bf16[512,512]{1,0:T(8,128)(2,1)S(1)} %slice.205), channel_id=1, source_target_pairs={{4,0},{8,4},{12,8},{16,12},{20,16},{24,20},{28,24},{5,1},{9,5},{13... | collective-permute-start | bytes 1572872 | tf_op jit(solution)/shard_map/ppermute | solution.py:14
  281.6 70.0 %reduce-scatter.11.cloned.1.call-start = ((), (), s32[]{:S(2)}) async-start(), calls=%async_computation.11 | async-start | bytes 4423680 | tf_op jit(solution)/shard_map/reduce_scatter | solution.py:237
  283.3 21.2 %copy-start.29 = (f32[128,128]{1,0:T(8,128)S(1)}, f32[128,128]{1,0:T(8,128)}, u32[]{:S(2)}) copy-start(f32[128,128]{1,0:T(8,128)} %copy-done.28) | copy-start | bytes 196612
  283.3 22.1 %copy-start.22 = (f32[128,128]{1,0:T(8,128)S(1)}, f32[128,128]{1,0:T(8,128)}, u32[]{:S(2)}) copy-start(f32[128,128]{1,0:T(8,128)} %copy-done.21) | copy-start | bytes 196612
  283.3 22.1 %copy-start.40 = (f32[2,1,128]{2,1,0:T(1,128)S(1)}, f32[2,1,128]{2,1,0:T(1,128)}, u32[]{:S(2)}) copy-start(f32[2,1,128]{2,1,0:T(1,128)} %copy-done.39) | copy-start | bytes 3076
  283.3 22.1 %copy-start.50 = (f32[128]{0:T(128)S(1)}, f32[128]{0:T(128)}, u32[]{:S(2)}) copy-start(f32[128]{0:T(128)} %copy-done.49) | copy-start | bytes 1540
  284.1 24.1 %copy-start.53 = (f32[128]{0:T(128)S(1)}, f32[128]{0:T(128)}, u32[]{:S(2)}) copy-start(f32[128]{0:T(128)} %copy-done.52) | copy-start | bytes 1540
  304.4 6.7 copy-start.33
  308.1 3.0 copy-start.35
  311.2 75.9 %reduce-scatter.13.cloned.1.call-start = ((), (), s32[]{:S(2)}) async-start(), calls=%async_computation.12 | async-start | bytes 2949120 | tf_op jit(solution)/shard_map/reduce_scatter | solution.py:240
  314.4 144.7 %reduce-scatter.17.cloned.1.call-start = ((), (), s32[]{:S(2)}) async-start(), calls=%async_computation.14 | async-start | bytes 9953280 | tf_op jit(solution)/shard_map/reduce_scatter | solution.py:246
  321.4 260.4 %reduce-scatter.15.cloned.1.call-start = ((), (), s32[]{:S(2)}) async-start(), calls=%async_computation.13 | async-start | bytes 19906560 | tf_op jit(solution)/shard_map/reduce_scatter | solution.py:243
  331.1 273.9 %reduce-scatter.19.cloned.1.call-start = ((), (), s32[]{:S(2)}) async-start(), calls=%async_computation.16 | async-start | bytes 368640
  336.2 379.3 %all-gather.17.cloned.1.call-start = ((), (), s32[]{:S(2)}) async-start(), calls=%async_computation.15 | async-start | bytes 7962624 | tf_op jit(solution)/shard_map/all_gather | solution.py:257
  351.7 584.8 %all-reduce.5.cloned.1.call-start = ((), (), s32[]{:S(2)}) async-start(), calls=%async_computation.17 | async-start | bytes 13123584 | tf_op jit(solution)/shard_map/psum | solution.py:258
  581.8 7.8 copy-start.54
  938.7 6.0 copy-start.11
  (26 other events, 30.6 us)
Sparse Core Ops, SparseCore 0:
  9.5 33.4 all-gather.8
  44.6 24.0 all-gather.10
  70.2 101.0 all-gather.12
  172.7 55.8 all-gather.14
  281.8 21.6 reduce-scatter.8
  311.3 40.3 reduce-scatter.10
  354.2 32.8 reduce-scatter.12
  390.2 68.8 reduce-scatter.16
  461.7 120.0 reduce-scatter.14
  584.7 20.2 reduce-scatter.18
  607.2 108.3 all-gather.16
  719.9 216.5 all-reduce.4
